TPU v7x, 32 devices: a whole 2x2x4 slice. The times are simulated.
32 devices in a mesh: row: 4 (over y, x), col: 2 (over core), vol: 4 (over z).
Axes of the slice: x: 2, y: 2, z: 4, core: 2. Of those that a mesh axis runs over, the one named last changes fastest.
Arguments:
- panel: bfloat16 [512, 131072], P('row', ('col', 'vol')), may hold values from -0.015625 to 0.015625
- density: float32 [32, 131072], P(None, ('col', 'vol')), may hold values from -6 to 6
- source: float32 [32, 32, 16, 512], P(None, 'row', 'col', 'vol'), may hold values from -6 to 6
- class_index: int32 [32, 16, 512], P('row', 'col', 'vol'), may hold values from 0 to 15
- class_values: float32 [16], replicated, may hold values from 0.2 to 5
- trace_count: int32 [4, 8], P('row'), may hold values from 1 to 64, 128 in all within a row
- trace_cell: int32 [4, 8, 64], P('row'), may hold values from 0 to 8191
Outputs:
- density_out: float32 [32, 131072], P(None, ('col', 'vol'))
- volume_out: float32 [32, 32, 16, 512], P(None, 'row', 'col', 'vol')
Inputs may be any that keep to these rules, and one draw needn't show every extreme that they name: `trace_count`: in each row r, the counts of the 8 blocks are 1 or more and sum to 128, so that every target of row tile r has exactly one live slot; the largest count of each row is 64. `trace_cell`: only the first trace_count[r, j] slots of block j are read; two slots may hit one cell.
All inputs are finite; a program needn't handle non-finite values.
Results may differ from a plain program's by a relative error of at most 0.00035.
Values may be sent and summed in bfloat16 or wider, within the bound.
No kernel may reach another device: no remote copies, remote signals or barrier semaphores. Data moves between devices by JAX's collectives and lax.ppermute only.
A program may use at most 128 MiB of HBM per device.

v0:
```python
import math
import jax
import jax.numpy as jnp
from jax import lax
from jax.sharding import PartitionSpec as P

SWEEPS = 4
OUTER = 2
MASS_TERM = 0.1
RELAXATION = 0.5
SPECTRUM_LOW = 0.1
SPECTRUM_HIGH = 2.0


def padded_2(value, sides, width):
    for axis, dim in sides:
        size, length = (lax.axis_size(axis), value.shape[dim])
        up = [(i, (i + 1) % size) for i in range(size - 1)]
        down = [(j, i) for i, j in up]
        last = lax.slice_in_dim(value, length - width, length, axis=dim)
        first = lax.slice_in_dim(value, 0, width, axis=dim)
        before = lax.ppermute(last, axis, up)
        after = lax.ppermute(first, axis, down)
        value = jnp.concatenate([before, value, after], axis=dim)
    return value


def relax_factors(count):
    middle = (SPECTRUM_HIGH + SPECTRUM_LOW) / 2.0
    spread = (SPECTRUM_HIGH - SPECTRUM_LOW) / 2.0
    return [
        1.0 / (middle + spread * math.cos(math.pi * (2 * order + 1) / (2 * count)))
        for order in range(count)
    ]


def neighbours(padded):
    center = padded[..., 1:-1, 1:-1, 1:-1]
    beside_all = padded[..., 2:, 1:-1, 1:-1] + padded[..., :-2, 1:-1, 1:-1]
    beside_all = beside_all + padded[..., 1:-1, 2:, 1:-1] + padded[..., 1:-1, :-2, 1:-1]
    beside_all = beside_all + padded[..., 1:-1, 1:-1, 2:] + padded[..., 1:-1, 1:-1, :-2]
    return (center, beside_all)


def local(panel, density, source, class_index, class_values, trace_count, trace_cell):
    factors = relax_factors(SWEEPS)
    classes = jnp.arange(class_values.shape[0], dtype=jnp.int32)
    conduct = jnp.sum(
        jnp.where(
            class_index[None] == classes[:, None, None, None],
            class_values[:, None, None, None],
            jnp.float32(0.0),
        ),
        axis=0,
    )
    diagonal = MASS_TERM + 6.0 * conduct
    counts = trace_count[0]
    block_index = lax.axis_index(("col", "vol"))
    offsets = jnp.cumsum(counts) - counts
    target_rows = panel.shape[0]
    slot_count = trace_cell.shape[2]
    slot_ids = jnp.arange(slot_count, dtype=jnp.int32)
    target_ids = jnp.arange(target_rows, dtype=jnp.int32)
    own_count = lax.dynamic_index_in_dim(counts, block_index, keepdims=False)
    first_target = lax.dynamic_index_in_dim(offsets, block_index, keepdims=False)
    cell_ids = lax.dynamic_index_in_dim(trace_cell[0], block_index, keepdims=False)
    live_slots = slot_ids < own_count
    select = (
        ((first_target + slot_ids)[:, None] == target_ids[None, :]) & live_slots[:, None]
    ).astype(jnp.float32)
    volume = jnp.zeros(source.shape, jnp.float32)
    field_shape = volume.shape
    share_width = density.shape[1] // lax.axis_size("row")
    share_state = lax.dynamic_slice_in_dim(
        density, lax.axis_index("row") * share_width, share_width, 1
    )
    rounded = density.astype(jnp.bfloat16)
    lead = field_shape[0]
    for iteration in range(OUTER):
        partial_value = lax.dot_general(
            rounded, panel, (((1,), (1,)), ((), ())), preferred_element_type=jnp.float32
        )
        potential = lax.psum(partial_value, ("col", "vol"))
        slot_values = jnp.dot(potential, select.T, precision=lax.Precision.HIGHEST)
        right_side = source.reshape(lead, -1).at[:, cell_ids].add(slot_values).reshape(field_shape)
        relax_volume = volume
        for factor in factors:
            padded = padded_2(relax_volume, (("row", 1), ("col", 2), ("vol", 3)), 1)
            center, beside_all = neighbours(padded)
            relax_volume = (
                center + factor * (right_side - diagonal * center + conduct * beside_all) / diagonal
            )
        volume = relax_volume
        mismatch = volume.reshape(lead, -1)[:, cell_ids] - slot_values
        own_fluxes = jnp.dot(mismatch, select, precision=lax.Precision.HIGHEST)
        fluxes = lax.psum(own_fluxes, ("col", "vol"))
        update = jnp.dot(fluxes.astype(jnp.bfloat16), panel, preferred_element_type=jnp.float32)
        share_state = share_state + RELAXATION * lax.psum_scatter(
            update, "row", scatter_dimension=1, tiled=True
        )
        if iteration + 1 < OUTER:
            rounded = lax.all_gather(share_state.astype(jnp.bfloat16), "row", axis=1, tiled=True)
    density = lax.all_gather(share_state, "row", axis=1, tiled=True)
    return (density, volume)


def solution(mesh):
    placed = (
        P("row", ("col", "vol")),
        P(None, ("col", "vol")),
        P(None, "row", "col", "vol"),
        P("row", "col", "vol"),
        P(),
        P("row", None),
        P("row", None, None),
    )
    return jax.shard_map(
        local,
        mesh=mesh,
        in_specs=placed,
        out_specs=(P(None, ("col", "vol")), P(None, "row", "col", "vol")),
        check_vma=False,
    )
```

profile of v0, /device:TPU:0, one launch (start us, length us, event | category | flops | bytes accessed | tf_op | source)
XLA Modules:
  0.0 584.9 jit_solution(7050335987216102525)
XLA Ops:
  8.5 5.5 collective-permute-start.1
  17.0 4.3 fusion.79
  22.7 28.9 %psum.28 = f32[32,128]{1,0:T(8,128)S(1)} all-reduce(f32[32,128]{1,0:T(8,128)S(1)} %fusion.79), channel_id=1, replica_groups=mesh['row'=4,'col'=2,'vol'=4] {'col','vol'}, use_global_device_ids=true, to_apply=%region_0.1 | all-reduce | flops 4096 | bytes 32768 | tf_op jit(solution)/shard_map/psum | solution.py:83
  67.1 4.6 collective-permute-start.5
  75.2 4.5 copy.121
  79.6 5.0 scatter_fusion
  95.4 5.0 collective-permute-start.7
  117.0 4.6 collective-permute-start.11
  129.7 5.2 collective-permute-start.13
  138.9 3.5 collective-permute-start.15
  150.7 5.0 collective-permute-start.17
  164.1 5.9 %collective-permute-start.19 = (f32[32,1,8,128]{3,0,2,1:T(8,128)S(1)}, f32[32,1,8,128]{3,0,2,1:T(8,128)S(1)}, u32[]{:S(2)}, u32[]{:S(2)}) collective-permute-start(f32[32,1,8,128]{3,0,2,1:T(8,128)S(1)} %get-tuple-element.46), channel_id=1, source_target_pairs={{0,8},{8,16},{16,24},{1,9},{9,17},{17,25},{2,10},{10,18},{18,26},{... | collective-permute-start | bytes 393224 | tf_op jit(solution)/shard_map/ppermute | solution.py:22
  187.1 4.9 collective-permute-start.23
  204.7 29.4 %psum.29 = bf16[32,128]{1,0:T(8,128)(2,1)S(1)} all-reduce(f32[32,128]{1,0:T(8,128)S(1)} %fusion.87), channel_id=1, replica_groups=mesh['row'=4,'col'=2,'vol'=4] {'col','vol'}, use_global_device_ids=true, to_apply=%region_4.5 | all-reduce | flops 4096 | bytes 24576 | tf_op jit(solution)/shard_map/psum | solution.py:96
  234.1 4.2 fusion.122
  238.4 38.0 %reduce-scatter.3.cloned.1.call-done = f32[32,4096]{1,0:T(8,128)} async-done(((f32[32,16384]{1,0:T(8,128)}), f32[32,4096]{1,0:T(8,128)}) %reduce-scatter.3.cloned.1.call-update) | async-done | bytes 524304 | tf_op jit(solution)/shard_map/reduce_scatter | solution.py:98
  279.7 4.6 collective-permute-start.25
  297.1 3.4 collective-permute-start.29
  311.1 4.0 fusion.120
  315.1 27.5 %psum.30 = f32[32,128]{1,0:T(8,128)S(1)} all-reduce(f32[32,128]{1,0:T(8,128)S(1)} %fusion.120), channel_id=1, replica_groups=mesh['row'=4,'col'=2,'vol'=4] {'col','vol'}, use_global_device_ids=true, to_apply=%region_6.7 | all-reduce | flops 4096 | bytes 32768 | tf_op jit(solution)/shard_map/psum | solution.py:83
  342.9 5.0 scatter_fusion.1
  355.0 6.1 %collective-permute-start.31 = (f32[32,1,8,128]{3,0,2,1:T(8,128)S(1)}, f32[32,1,8,128]{3,0,2,1:T(8,128)S(1)}, u32[]{:S(2)}, u32[]{:S(2)}) collective-permute-start(f32[32,1,8,128]{3,0,2,1:T(8,128)S(1)} %get-tuple-element.42), channel_id=1, source_target_pairs={{0,8},{8,16},{16,24},{1,9},{9,17},{17,25},{2,10},{10,18},{18,26},{... | collective-permute-start | bytes 393224 | tf_op jit(solution)/shard_map/ppermute | solution.py:22
  378.1 4.6 collective-permute-start.35
  390.8 5.9 %collective-permute-start.37 = (f32[32,1,8,128]{3,0,2,1:T(8,128)S(1)}, f32[32,1,8,128]{3,0,2,1:T(8,128)S(1)}, u32[]{:S(2)}, u32[]{:S(2)}) collective-permute-start(f32[32,1,8,128]{3,0,2,1:T(8,128)S(1)} %get-tuple-element.40), channel_id=1, source_target_pairs={{0,8},{8,16},{16,24},{1,9},{9,17},{17,25},{2,10},{10,18},{18,26},{... | collective-permute-start | bytes 393224 | tf_op jit(solution)/shard_map/ppermute | solution.py:22
  412.4 5.0 collective-permute-start.41
  425.8 5.9 %collective-permute-start.43 = (f32[32,1,8,128]{3,0,2,1:T(8,128)S(1)}, f32[32,1,8,128]{3,0,2,1:T(8,128)S(1)}, u32[]{:S(2)}, u32[]{:S(2)}) collective-permute-start(f32[32,1,8,128]{3,0,2,1:T(8,128)S(1)} %get-tuple-element.38), channel_id=1, source_target_pairs={{0,8},{8,16},{16,24},{1,9},{9,17},{17,25},{2,10},{10,18},{18,26},{... | collective-permute-start | bytes 393224 | tf_op jit(solution)/shard_map/ppermute | solution.py:22
  435.7 3.3 collective-permute-start.45
  448.3 4.9 collective-permute-start.47
  466.0 29.4 %psum.31 = bf16[32,128]{1,0:T(8,128)(2,1)S(1)} all-reduce(f32[32,128]{1,0:T(8,128)S(1)} %fusion.83), channel_id=1, replica_groups=mesh['row'=4,'col'=2,'vol'=4] {'col','vol'}, use_global_device_ids=true, to_apply=%region_8.9 | all-reduce | flops 4096 | bytes 24576 | tf_op jit(solution)/shard_map/psum | solution.py:96
  495.3 4.2 fusion.121
  499.6 38.0 %reduce-scatter.5.cloned.1.call-done = f32[32,4096]{1,0:T(8,128)} async-done(((f32[32,16384]{1,0:T(8,128)}), f32[32,4096]{1,0:T(8,128)}) %reduce-scatter.5.cloned.1.call-update) | async-done | bytes 524304 | tf_op jit(solution)/shard_map/reduce_scatter | solution.py:98
  541.3 33.8 %all-gather.5.cloned.1.call-done = f32[32,16384]{1,0:T(8,128)} async-done(((f32[32,4096]{1,0:T(8,128)}), f32[32,16384]{1,0:T(8,128)}) %all-gather.5.cloned.1.call-update) | async-done | bytes 2097168 | tf_op jit(solution)/shard_map/all_gather | solution.py:103
  (239 shorter events, 225.9 us)
Async XLA Ops:
  7.2 269.2 %reduce-scatter.3.cloned.1.call-start = ((), (), s32[]{:S(2)}) async-start(), calls=%async_computation.2 | async-start | bytes 2621440 | tf_op jit(solution)/shard_map/reduce_scatter | solution.py:98
  7.2 45.0 %collective-permute-start = (f32[32,1,8,128]{3,0,2,1:T(8,128)S(1)}, f32[32,1,8,128]{3,0,2,1:T(8,128)S(1)}, u32[]{:S(2)}, u32[]{:S(2)}) collective-permute-start(f32[32,1,8,128]{3,0,2,1:T(8,128)S(1)} %broadcast.65), channel_id=1, source_target_pairs={{8,0},{16,8},{24,16},{9,1},{17,9},{25,17},{10,2},{18,10},{26,18},{... | collective-permute-start | bytes 393224 | tf_op jit(solution)/shard_map/ppermute | solution.py:23
  8.5 43.7 %collective-permute-start.1 = (f32[32,1,8,128]{3,0,2,1:T(8,128)S(1)}, f32[32,1,8,128]{3,0,2,1:T(8,128)S(1)}, u32[]{:S(2)}, u32[]{:S(2)}) collective-permute-start(f32[32,1,8,128]{3,0,2,1:T(8,128)S(1)} %broadcast.65), channel_id=1, source_target_pairs={{0,8},{8,16},{16,24},{1,9},{9,17},{17,25},{2,10},{10,18},{18,26},{... | collective-permute-start | bytes 393224 | tf_op jit(solution)/shard_map/ppermute | solution.py:22
  63.3 24.1 %collective-permute-start.4 = (f32[32,10,10,1]{0,2,3,1:T(8,128)S(1)}, f32[32,10,10,1]{0,2,3,1:T(8,128)S(1)}, u32[]{:S(2)}, u32[]{:S(2)}) collective-permute-start(f32[32,10,10,1]{0,2,3,1:T(8,128)S(1)} %copy.75), channel_id=1, source_target_pairs={{1,0},{2,1},{3,2},{5,4},{6,5},{7,6},{9,8},{10,9},{11,10},{13,12},{... | collective-permute-start | bytes 38408 | tf_op jit(solution)/shard_map/ppermute | solution.py:23
  67.1 22.3 %collective-permute-start.5 = (f32[32,10,10,1]{0,2,3,1:T(8,128)S(1)}, f32[32,10,10,1]{0,2,3,1:T(8,128)S(1)}, u32[]{:S(2)}, u32[]{:S(2)}) collective-permute-start(f32[32,10,10,1]{0,2,3,1:T(8,128)S(1)} %copy.77), channel_id=1, source_target_pairs={{0,1},{1,2},{2,3},{4,5},{5,6},{6,7},{8,9},{9,10},{10,11},{12,13},{... | collective-permute-start | bytes 38408 | tf_op jit(solution)/shard_map/ppermute | solution.py:22
  94.1 7.8 %collective-permute-start.6 = (f32[32,1,8,128]{3,0,2,1:T(8,128)S(1)}, f32[32,1,8,128]{3,0,2,1:T(8,128)S(1)}, u32[]{:S(2)}, u32[]{:S(2)}) collective-permute-start(f32[32,1,8,128]{3,0,2,1:T(8,128)S(1)} %get-tuple-element.51), channel_id=1, source_target_pairs={{8,0},{16,8},{24,16},{9,1},{17,9},{25,17},{10,2},{18,10},{26,18},{... | collective-permute-start | bytes 393224 | tf_op jit(solution)/shard_map/ppermute | solution.py:23
  95.4 7.7 %collective-permute-start.7 = (f32[32,1,8,128]{3,0,2,1:T(8,128)S(1)}, f32[32,1,8,128]{3,0,2,1:T(8,128)S(1)}, u32[]{:S(2)}, u32[]{:S(2)}) collective-permute-start(f32[32,1,8,128]{3,0,2,1:T(8,128)S(1)} %get-tuple-element.50), channel_id=1, source_target_pairs={{0,8},{8,16},{16,24},{1,9},{9,17},{17,25},{2,10},{10,18},{18,26},{... | collective-permute-start | bytes 393224 | tf_op jit(solution)/shard_map/ppermute | solution.py:22
  113.3 8.3 %collective-permute-start.10 = (f32[32,10,10,1]{0,2,3,1:T(8,128)S(1)}, f32[32,10,10,1]{0,2,3,1:T(8,128)S(1)}, u32[]{:S(2)}, u32[]{:S(2)}) collective-permute-start(f32[32,10,10,1]{0,2,3,1:T(8,128)S(1)} %copy.80), channel_id=1, source_target_pairs={{1,0},{2,1},{3,2},{5,4},{6,5},{7,6},{9,8},{10,9},{11,10},{13,12},{... | collective-permute-start | bytes 38408 | tf_op jit(solution)/shard_map/ppermute | solution.py:23
  128.4 7.9 %collective-permute-start.12 = (f32[32,1,8,128]{3,0,2,1:T(8,128)S(1)}, f32[32,1,8,128]{3,0,2,1:T(8,128)S(1)}, u32[]{:S(2)}, u32[]{:S(2)}) collective-permute-start(f32[32,1,8,128]{3,0,2,1:T(8,128)S(1)} %get-tuple-element.49), channel_id=1, source_target_pairs={{8,0},{16,8},{24,16},{9,1},{17,9},{25,17},{10,2},{18,10},{26,18},{... | collective-permute-start | bytes 393224 | tf_op jit(solution)/shard_map/ppermute | solution.py:23
  129.7 7.8 %collective-permute-start.13 = (f32[32,1,8,128]{3,0,2,1:T(8,128)S(1)}, f32[32,1,8,128]{3,0,2,1:T(8,128)S(1)}, u32[]{:S(2)}, u32[]{:S(2)}) collective-permute-start(f32[32,1,8,128]{3,0,2,1:T(8,128)S(1)} %get-tuple-element.48), channel_id=1, source_target_pairs={{0,8},{8,16},{16,24},{1,9},{9,17},{17,25},{2,10},{10,18},{18,26},{... | collective-permute-start | bytes 393224 | tf_op jit(solution)/shard_map/ppermute | solution.py:22
  148.4 7.3 %collective-permute-start.16 = (f32[32,10,10,1]{0,2,3,1:T(8,128)S(1)}, f32[32,10,10,1]{0,2,3,1:T(8,128)S(1)}, u32[]{:S(2)}, u32[]{:S(2)}) collective-permute-start(f32[32,10,10,1]{0,2,3,1:T(8,128)S(1)} %copy.85), channel_id=1, source_target_pairs={{1,0},{2,1},{3,2},{5,4},{6,5},{7,6},{9,8},{10,9},{11,10},{13,12},{... | collective-permute-start | bytes 38408 | tf_op jit(solution)/shard_map/ppermute | solution.py:23
  150.7 7.2 %collective-permute-start.17 = (f32[32,10,10,1]{0,2,3,1:T(8,128)S(1)}, f32[32,10,10,1]{0,2,3,1:T(8,128)S(1)}, u32[]{:S(2)}, u32[]{:S(2)}) collective-permute-start(f32[32,10,10,1]{0,2,3,1:T(8,128)S(1)} %copy.87), channel_id=1, source_target_pairs={{0,1},{1,2},{2,3},{4,5},{5,6},{6,7},{8,9},{9,10},{10,11},{12,13},{... | collective-permute-start | bytes 38408 | tf_op jit(solution)/shard_map/ppermute | solution.py:22
  162.8 8.7 %collective-permute-start.18 = (f32[32,1,8,128]{3,0,2,1:T(8,128)S(1)}, f32[32,1,8,128]{3,0,2,1:T(8,128)S(1)}, u32[]{:S(2)}, u32[]{:S(2)}) collective-permute-start(f32[32,1,8,128]{3,0,2,1:T(8,128)S(1)} %get-tuple-element.47), channel_id=1, source_target_pairs={{8,0},{16,8},{24,16},{9,1},{17,9},{25,17},{10,2},{18,10},{26,18},{... | collective-permute-start | bytes 393224 | tf_op jit(solution)/shard_map/ppermute | solution.py:23
  164.1 8.5 %collective-permute-start.19 = (f32[32,1,8,128]{3,0,2,1:T(8,128)S(1)}, f32[32,1,8,128]{3,0,2,1:T(8,128)S(1)}, u32[]{:S(2)}, u32[]{:S(2)}) collective-permute-start(f32[32,1,8,128]{3,0,2,1:T(8,128)S(1)} %get-tuple-element.46), channel_id=1, source_target_pairs={{0,8},{8,16},{16,24},{1,9},{9,17},{17,25},{2,10},{10,18},{18,26},{... | collective-permute-start | bytes 393224 | tf_op jit(solution)/shard_map/ppermute | solution.py:22
  183.3 8.6 %collective-permute-start.22 = (f32[32,10,10,1]{0,2,3,1:T(8,128)S(1)}, f32[32,10,10,1]{0,2,3,1:T(8,128)S(1)}, u32[]{:S(2)}, u32[]{:S(2)}) collective-permute-start(f32[32,10,10,1]{0,2,3,1:T(8,128)S(1)} %copy.90), channel_id=1, source_target_pairs={{1,0},{2,1},{3,2},{5,4},{6,5},{7,6},{9,8},{10,9},{11,10},{13,12},{... | collective-permute-start | bytes 38408 | tf_op jit(solution)/shard_map/ppermute | solution.py:23
  187.1 7.1 %collective-permute-start.23 = (f32[32,10,10,1]{0,2,3,1:T(8,128)S(1)}, f32[32,10,10,1]{0,2,3,1:T(8,128)S(1)}, u32[]{:S(2)}, u32[]{:S(2)}) collective-permute-start(f32[32,10,10,1]{0,2,3,1:T(8,128)S(1)} %copy.92), channel_id=1, source_target_pairs={{0,1},{1,2},{2,3},{4,5},{5,6},{6,7},{8,9},{9,10},{10,11},{12,13},{... | collective-permute-start | bytes 38408 | tf_op jit(solution)/shard_map/ppermute | solution.py:22
  238.3 72.8 %all-gather.3.cloned.1.call-start = ((), (), s32[]{:S(2)}) async-start(), calls=%async_computation.3 | async-start | bytes 1310720 | tf_op jit(solution)/shard_map/all_gather | solution.py:102
  278.4 259.3 %reduce-scatter.5.cloned.1.call-start = ((), (), s32[]{:S(2)}) async-start(), calls=%async_computation.4 | async-start | bytes 2621440 | tf_op jit(solution)/shard_map/reduce_scatter | solution.py:98
  279.7 7.1 %collective-permute-start.25 = (f32[32,1,8,128]{3,0,2,1:T(8,128)S(1)}, f32[32,1,8,128]{3,0,2,1:T(8,128)S(1)}, u32[]{:S(2)}, u32[]{:S(2)}) collective-permute-start(f32[32,1,8,128]{3,0,2,1:T(8,128)S(1)} %get-tuple-element.44), channel_id=1, source_target_pairs={{0,8},{8,16},{16,24},{1,9},{9,17},{17,25},{2,10},{10,18},{18,26},{... | collective-permute-start | bytes 393224 | tf_op jit(solution)/shard_map/ppermute | solution.py:22
  297.1 7.3 %collective-permute-start.29 = (f32[32,10,10,1]{0,2,3,1:T(8,128)S(1)}, f32[32,10,10,1]{0,2,3,1:T(8,128)S(1)}, u32[]{:S(2)}, u32[]{:S(2)}) collective-permute-start(f32[32,10,10,1]{0,2,3,1:T(8,128)S(1)} %copy.100), channel_id=1, source_target_pairs={{0,1},{1,2},{2,3},{4,5},{5,6},{6,7},{8,9},{9,10},{10,11},{12,13},{... | collective-permute-start | bytes 38408 | tf_op jit(solution)/shard_map/ppermute | solution.py:22
  353.7 9.2 %collective-permute-start.30 = (f32[32,1,8,128]{3,0,2,1:T(8,128)S(1)}, f32[32,1,8,128]{3,0,2,1:T(8,128)S(1)}, u32[]{:S(2)}, u32[]{:S(2)}) collective-permute-start(f32[32,1,8,128]{3,0,2,1:T(8,128)S(1)} %get-tuple-element.43), channel_id=1, source_target_pairs={{8,0},{16,8},{24,16},{9,1},{17,9},{25,17},{10,2},{18,10},{26,18},{... | collective-permute-start | bytes 393224 | tf_op jit(solution)/shard_map/ppermute | solution.py:23
  355.0 9.1 %collective-permute-start.31 = (f32[32,1,8,128]{3,0,2,1:T(8,128)S(1)}, f32[32,1,8,128]{3,0,2,1:T(8,128)S(1)}, u32[]{:S(2)}, u32[]{:S(2)}) collective-permute-start(f32[32,1,8,128]{3,0,2,1:T(8,128)S(1)} %get-tuple-element.42), channel_id=1, source_target_pairs={{0,8},{8,16},{16,24},{1,9},{9,17},{17,25},{2,10},{10,18},{18,26},{... | collective-permute-start | bytes 393224 | tf_op jit(solution)/shard_map/ppermute | solution.py:22
  374.4 8.3 %collective-permute-start.34 = (f32[32,10,10,1]{0,2,3,1:T(8,128)S(1)}, f32[32,10,10,1]{0,2,3,1:T(8,128)S(1)}, u32[]{:S(2)}, u32[]{:S(2)}) collective-permute-start(f32[32,10,10,1]{0,2,3,1:T(8,128)S(1)} %copy.103), channel_id=1, source_target_pairs={{1,0},{2,1},{3,2},{5,4},{6,5},{7,6},{9,8},{10,9},{11,10},{13,12},{... | collective-permute-start | bytes 38408 | tf_op jit(solution)/shard_map/ppermute | solution.py:23
  389.5 8.6 %collective-permute-start.36 = (f32[32,1,8,128]{3,0,2,1:T(8,128)S(1)}, f32[32,1,8,128]{3,0,2,1:T(8,128)S(1)}, u32[]{:S(2)}, u32[]{:S(2)}) collective-permute-start(f32[32,1,8,128]{3,0,2,1:T(8,128)S(1)} %get-tuple-element.41), channel_id=1, source_target_pairs={{8,0},{16,8},{24,16},{9,1},{17,9},{25,17},{10,2},{18,10},{26,18},{... | collective-permute-start | bytes 393224 | tf_op jit(solution)/shard_map/ppermute | solution.py:23
  390.8 8.4 %collective-permute-start.37 = (f32[32,1,8,128]{3,0,2,1:T(8,128)S(1)}, f32[32,1,8,128]{3,0,2,1:T(8,128)S(1)}, u32[]{:S(2)}, u32[]{:S(2)}) collective-permute-start(f32[32,1,8,128]{3,0,2,1:T(8,128)S(1)} %get-tuple-element.40), channel_id=1, source_target_pairs={{0,8},{8,16},{16,24},{1,9},{9,17},{17,25},{2,10},{10,18},{18,26},{... | collective-permute-start | bytes 393224 | tf_op jit(solution)/shard_map/ppermute | solution.py:22
  410.1 7.4 %collective-permute-start.40 = (f32[32,10,10,1]{0,2,3,1:T(8,128)S(1)}, f32[32,10,10,1]{0,2,3,1:T(8,128)S(1)}, u32[]{:S(2)}, u32[]{:S(2)}) collective-permute-start(f32[32,10,10,1]{0,2,3,1:T(8,128)S(1)} %copy.108), channel_id=1, source_target_pairs={{1,0},{2,1},{3,2},{5,4},{6,5},{7,6},{9,8},{10,9},{11,10},{13,12},{... | collective-permute-start | bytes 38408 | tf_op jit(solution)/shard_map/ppermute | solution.py:23
  412.4 7.3 %collective-permute-start.41 = (f32[32,10,10,1]{0,2,3,1:T(8,128)S(1)}, f32[32,10,10,1]{0,2,3,1:T(8,128)S(1)}, u32[]{:S(2)}, u32[]{:S(2)}) collective-permute-start(f32[32,10,10,1]{0,2,3,1:T(8,128)S(1)} %copy.110), channel_id=1, source_target_pairs={{0,1},{1,2},{2,3},{4,5},{5,6},{6,7},{8,9},{9,10},{10,11},{12,13},{... | collective-permute-start | bytes 38408 | tf_op jit(solution)/shard_map/ppermute | solution.py:22
  424.5 8.7 %collective-permute-start.42 = (f32[32,1,8,128]{3,0,2,1:T(8,128)S(1)}, f32[32,1,8,128]{3,0,2,1:T(8,128)S(1)}, u32[]{:S(2)}, u32[]{:S(2)}) collective-permute-start(f32[32,1,8,128]{3,0,2,1:T(8,128)S(1)} %get-tuple-element.39), channel_id=1, source_target_pairs={{8,0},{16,8},{24,16},{9,1},{17,9},{25,17},{10,2},{18,10},{26,18},{... | collective-permute-start | bytes 393224 | tf_op jit(solution)/shard_map/ppermute | solution.py:23
  425.8 8.5 %collective-permute-start.43 = (f32[32,1,8,128]{3,0,2,1:T(8,128)S(1)}, f32[32,1,8,128]{3,0,2,1:T(8,128)S(1)}, u32[]{:S(2)}, u32[]{:S(2)}) collective-permute-start(f32[32,1,8,128]{3,0,2,1:T(8,128)S(1)} %get-tuple-element.38), channel_id=1, source_target_pairs={{0,8},{8,16},{16,24},{1,9},{9,17},{17,25},{2,10},{10,18},{18,26},{... | collective-permute-start | bytes 393224 | tf_op jit(solution)/shard_map/ppermute | solution.py:22
  444.6 8.6 %collective-permute-start.46 = (f32[32,10,10,1]{0,2,3,1:T(8,128)S(1)}, f32[32,10,10,1]{0,2,3,1:T(8,128)S(1)}, u32[]{:S(2)}, u32[]{:S(2)}) collective-permute-start(f32[32,10,10,1]{0,2,3,1:T(8,128)S(1)} %copy.113), channel_id=1, source_target_pairs={{1,0},{2,1},{3,2},{5,4},{6,5},{7,6},{9,8},{10,9},{11,10},{13,12},{... | collective-permute-start | bytes 38408 | tf_op jit(solution)/shard_map/ppermute | solution.py:23
  448.3 7.1 %collective-permute-start.47 = (f32[32,10,10,1]{0,2,3,1:T(8,128)S(1)}, f32[32,10,10,1]{0,2,3,1:T(8,128)S(1)}, u32[]{:S(2)}, u32[]{:S(2)}) collective-permute-start(f32[32,10,10,1]{0,2,3,1:T(8,128)S(1)} %copy.115), channel_id=1, source_target_pairs={{0,1},{1,2},{2,3},{4,5},{5,6},{6,7},{8,9},{9,10},{10,11},{12,13},{... | collective-permute-start | bytes 38408 | tf_op jit(solution)/shard_map/ppermute | solution.py:22
  499.6 75.6 %all-gather.5.cloned.1.call-start = ((), (), s32[]{:S(2)}) async-start(), calls=%async_computation.5 | async-start | bytes 2621440 | tf_op jit(solution)/shard_map/all_gather | solution.py:103
  (45 other events, 235.6 us)
Sparse Core Ops, SparseCore 0:
  238.4 37.9 reduce-scatter.2
  278.8 26.9 all-gather.2
  499.7 37.9 reduce-scatter.4
  539.9 35.1 all-gather.4
where the time goes:
time: 595 us; the launch traced here: 585 us
  waiting for transfers between devices  140 us (24%)
  starting transfers between devices  137 us (23%)
  local copies, waits for them, and re-layouts  116 us (19%)
  blocking collectives  115 us (19%)
  other arithmetic  43.5 us (7%)
  matrix products  17.5 us (3%)
  between operations  15 us (3%)
    ppermute x24, starting transfers between devices, padded_2(): before = lax.ppermute(last, axis, up)  106 us
    reduce_scatter x2, waiting for transfers between devices, local(): lax.psum_scatter(update, 'row', scatter_dimension=1, tiled=True)  76.1 us
    psum x2, blocking collectives, local(): fluxes = lax.psum(own_fluxes, ('col', 'vol'))  58.7 us
    psum x2, blocking collectives, local(): potential = lax.psum(partial_value, ('col', 'vol'))  56.4 us
    slice x16, local copies, waits for them, and re-layouts, padded_2(): first = lax.slice_in_dim(value, 0, width, axis=dim)  37.9 us
    all_gather x1, waiting for transfers between devices, local(): density = lax.all_gather(share_state, 'row', axis=1, tiled=True)  33.8 us
    ppermute x24, starting transfers between devices, padded_2(): after = lax.ppermute(first, axis, down)  31.2 us
    add x7, other arithmetic, local(): center + factor * (right_side - diagonal * center + conduct * beside_all)...  20.6 us
  transfers between devices with their start and end apart: 52, of which 32 were waited for; matrix products, arithmetic and copies ran while one was open for 11% of the time, Pallas kernels for 0%

commit v1 on v0

--- a/solution.py
+++ b/solution.py
@@ -1,3 +1,4 @@
+import functools
 import math
 import jax
 import jax.numpy as jnp
@@ -10,6 +11,25 @@
 RELAXATION = 0.5
 SPECTRUM_LOW = 0.1
 SPECTRUM_HIGH = 2.0
+
+
+def expand_series_all(local_block, which_axis):
+    q_n = jax.lax.axis_size(which_axis)
+    parts_seen = []
+    for u in range(1, q_n):
+        parts_seen.append((u - 1, u))
+    low = parts_seen + [(q_n - 1, 0)]
+    current_arr = local_block
+    chunks = [current_arr]
+    for _ in range(q_n - 1):
+        current_arr = jax.lax.ppermute(current_arr, which_axis, low)
+        chunks += [current_arr]
+    mat_out = jnp.concatenate([*reversed(chunks)], axis=1)
+    reply = jax.lax.axis_index(which_axis)
+    return jnp.roll(mat_out, shift=(reply + 1) * current_arr.shape[1], axis=1)
+
+
+close_outputs_all = functools.partial(expand_series_all, which_axis="row")
 
 
 def padded_2(value, sides, width):
@@ -100,7 +120,7 @@
         )
         if iteration + 1 < OUTER:
             rounded = lax.all_gather(share_state.astype(jnp.bfloat16), "row", axis=1, tiled=True)
-    density = lax.all_gather(share_state, "row", axis=1, tiled=True)
+    density = close_outputs_all(share_state)
     return (density, volume)
 
 

time: 595 us -> 598 us (level)
    ppermute x0 -> x3, waiting for transfers between devices: none -> 37 us  [expand_series_all(): current_arr = jax.lax.ppermute(current_arr, which_axis, low)]
    all_gather x1 -> x0, waiting for transfers between devices: 33.8 us -> none  [local(): density = lax.all_gather(share_state, 'row', axis=1, tiled=True)]
    unnamed x54 -> x60, local copies, waits for them, and re-layouts: 13.8 us -> 11 us
  transfers between devices with their start and end apart: 52 -> 54, of which waited for: 32 -> 34; matrix products, arithmetic and copies ran while one was open for 11% -> 11% of each run, Pallas kernels for 0% -> 0%
where the time goes in v1:
time: 598 us; the launch traced here: 588 us
  waiting for transfers between devices  144 us (24%)
  starting transfers between devices  140 us (23%)
  local copies, waits for them, and re-layouts  115 us (19%)
  blocking collectives  115 us (19%)
  other arithmetic  42.7 us (7%)
  matrix products  17.5 us (3%)
  between operations  15.1 us (3%)
    ppermute x24, starting transfers between devices, padded_2(): before = lax.ppermute(last, axis, up)  106 us
    reduce_scatter x2, waiting for transfers between devices, local(): lax.psum_scatter(update, 'row', scatter_dimension=1, tiled=True)  76.1 us
    psum x2, blocking collectives, local(): fluxes = lax.psum(own_fluxes, ('col', 'vol'))  58.7 us
    psum x2, blocking collectives, local(): potential = lax.psum(partial_value, ('col', 'vol'))  56.4 us
    slice x16, local copies, waits for them, and re-layouts, padded_2(): first = lax.slice_in_dim(value, 0, width, axis=dim)  37.9 us
    ppermute x3, waiting for transfers between devices, expand_series_all(): current_arr = jax.lax.ppermute(current_arr, which_axis, low)  37 us
    ppermute x24, starting transfers between devices, padded_2(): after = lax.ppermute(first, axis, down)  31.2 us
    add x7, other arithmetic, local(): center + factor * (right_side - diagonal * center + conduct * beside_all)...  20.6 us
  transfers between devices with their start and end apart: 54, of which 34 were waited for; matrix products, arithmetic and copies ran while one was open for 11% of the time, Pallas kernels for 0%

profile of v1, /device:TPU:0, one launch (start us, length us, event | category | flops | bytes accessed | tf_op | source)
XLA Modules:
  0.0 588.2 jit_solution(12613226298876122367)
XLA Ops:
  8.5 5.5 collective-permute-start.1
  17.0 4.3 fusion.79
  22.7 28.9 %psum.28 = f32[32,128]{1,0:T(8,128)S(1)} all-reduce(f32[32,128]{1,0:T(8,128)S(1)} %fusion.79), channel_id=1, replica_groups=mesh['row'=4,'col'=2,'vol'=4] {'col','vol'}, use_global_device_ids=true, to_apply=%region_0.1 | all-reduce | flops 4096 | bytes 32768 | tf_op jit(solution)/shard_map/psum | solution.py:103
  67.1 4.6 collective-permute-start.5
  75.2 4.5 copy.121
  79.6 5.0 scatter_fusion
  95.4 5.0 collective-permute-start.7
  117.0 4.6 collective-permute-start.11
  129.7 5.2 collective-permute-start.13
  138.9 3.5 collective-permute-start.15
  150.7 5.0 collective-permute-start.17
  164.1 5.9 %collective-permute-start.19 = (f32[32,1,8,128]{3,0,2,1:T(8,128)S(1)}, f32[32,1,8,128]{3,0,2,1:T(8,128)S(1)}, u32[]{:S(2)}, u32[]{:S(2)}) collective-permute-start(f32[32,1,8,128]{3,0,2,1:T(8,128)S(1)} %get-tuple-element.46), channel_id=1, source_target_pairs={{0,8},{8,16},{16,24},{1,9},{9,17},{17,25},{2,10},{10,18},{18,26},{... | collective-permute-start | bytes 393224 | tf_op jit(solution)/shard_map/ppermute | solution.py:42
  187.1 4.9 collective-permute-start.23
  204.7 29.4 %psum.29 = bf16[32,128]{1,0:T(8,128)(2,1)S(1)} all-reduce(f32[32,128]{1,0:T(8,128)S(1)} %fusion.87), channel_id=1, replica_groups=mesh['row'=4,'col'=2,'vol'=4] {'col','vol'}, use_global_device_ids=true, to_apply=%region_4.5 | all-reduce | flops 4096 | bytes 24576 | tf_op jit(solution)/shard_map/psum | solution.py:116
  234.1 4.2 fusion.122
  238.4 38.0 %reduce-scatter.3.cloned.1.call-done = f32[32,4096]{1,0:T(8,128)} async-done(((f32[32,16384]{1,0:T(8,128)}), f32[32,4096]{1,0:T(8,128)}) %reduce-scatter.3.cloned.1.call-update) | async-done | bytes 524304 | tf_op jit(solution)/shard_map/reduce_scatter | solution.py:118
  279.7 4.6 collective-permute-start.25
  311.1 4.0 fusion.120
  315.1 27.5 %psum.30 = f32[32,128]{1,0:T(8,128)S(1)} all-reduce(f32[32,128]{1,0:T(8,128)S(1)} %fusion.120), channel_id=1, replica_groups=mesh['row'=4,'col'=2,'vol'=4] {'col','vol'}, use_global_device_ids=true, to_apply=%region_6.7 | all-reduce | flops 4096 | bytes 32768 | tf_op jit(solution)/shard_map/psum | solution.py:103
  342.9 5.0 scatter_fusion.1
  355.0 6.1 %collective-permute-start.31 = (f32[32,1,8,128]{3,0,2,1:T(8,128)S(1)}, f32[32,1,8,128]{3,0,2,1:T(8,128)S(1)}, u32[]{:S(2)}, u32[]{:S(2)}) collective-permute-start(f32[32,1,8,128]{3,0,2,1:T(8,128)S(1)} %get-tuple-element.42), channel_id=1, source_target_pairs={{0,8},{8,16},{16,24},{1,9},{9,17},{17,25},{2,10},{10,18},{18,26},{... | collective-permute-start | bytes 393224 | tf_op jit(solution)/shard_map/ppermute | solution.py:42
  378.1 4.6 collective-permute-start.35
  390.8 5.9 %collective-permute-start.37 = (f32[32,1,8,128]{3,0,2,1:T(8,128)S(1)}, f32[32,1,8,128]{3,0,2,1:T(8,128)S(1)}, u32[]{:S(2)}, u32[]{:S(2)}) collective-permute-start(f32[32,1,8,128]{3,0,2,1:T(8,128)S(1)} %get-tuple-element.40), channel_id=1, source_target_pairs={{0,8},{8,16},{16,24},{1,9},{9,17},{17,25},{2,10},{10,18},{18,26},{... | collective-permute-start | bytes 393224 | tf_op jit(solution)/shard_map/ppermute | solution.py:42
  412.4 5.0 collective-permute-start.41
  425.8 5.9 %collective-permute-start.43 = (f32[32,1,8,128]{3,0,2,1:T(8,128)S(1)}, f32[32,1,8,128]{3,0,2,1:T(8,128)S(1)}, u32[]{:S(2)}, u32[]{:S(2)}) collective-permute-start(f32[32,1,8,128]{3,0,2,1:T(8,128)S(1)} %get-tuple-element.38), channel_id=1, source_target_pairs={{0,8},{8,16},{16,24},{1,9},{9,17},{17,25},{2,10},{10,18},{18,26},{... | collective-permute-start | bytes 393224 | tf_op jit(solution)/shard_map/ppermute | solution.py:42
  448.3 4.9 collective-permute-start.47
  466.0 29.4 %psum.31 = bf16[32,128]{1,0:T(8,128)(2,1)S(1)} all-reduce(f32[32,128]{1,0:T(8,128)S(1)} %fusion.83), channel_id=1, replica_groups=mesh['row'=4,'col'=2,'vol'=4] {'col','vol'}, use_global_device_ids=true, to_apply=%region_8.9 | all-reduce | flops 4096 | bytes 24576 | tf_op jit(solution)/shard_map/psum | solution.py:116
  495.3 4.2 fusion.121
  499.6 38.1 %reduce-scatter.5.cloned.1.call-done = f32[32,4096]{1,0:T(8,128)} async-done(((f32[32,16384]{1,0:T(8,128)}), f32[32,4096]{1,0:T(8,128)}) %reduce-scatter.5.cloned.1.call-update) | async-done | bytes 524304 | tf_op jit(solution)/shard_map/reduce_scatter | solution.py:118
  540.4 12.9 %collective-permute-done.48 = f32[32,4096]{1,0:T(8,128)S(1)} collective-permute-done((f32[32,4096]{1,0:T(8,128)S(1)}, f32[32,4096]{1,0:T(8,128)S(1)}, u32[]{:S(2)}, u32[]{:S(2)}) %collective-permute-start.48) | collective-permute-done | bytes 524320 | tf_op jit(solution)/shard_map/ppermute | solution.py:25
  553.9 13.0 %collective-permute-done.49 = f32[32,4096]{1,0:T(8,128)S(1)} collective-permute-done((f32[32,4096]{1,0:T(8,128)S(1)}, f32[32,4096]{1,0:T(8,128)S(1)}, u32[]{:S(2)}, u32[]{:S(2)}) %collective-permute-start.49) | collective-permute-done | bytes 524320 | tf_op jit(solution)/shard_map/ppermute | solution.py:25
  568.5 11.1 %collective-permute-done.50 = f32[32,4096]{1,0:T(8,128)S(1)} collective-permute-done((f32[32,4096]{1,0:T(8,128)S(1)}, f32[32,4096]{1,0:T(8,128)S(1)}, u32[]{:S(2)}, u32[]{:S(2)}) %collective-permute-start.50) | collective-permute-done | bytes 524320 | tf_op jit(solution)/shard_map/ppermute | solution.py:25
  (250 shorter events, 232.5 us)
Async XLA Ops:
  7.2 269.2 %reduce-scatter.3.cloned.1.call-start = ((), (), s32[]{:S(2)}) async-start(), calls=%async_computation.2 | async-start | bytes 2621440 | tf_op jit(solution)/shard_map/reduce_scatter | solution.py:118
  7.2 45.0 %collective-permute-start = (f32[32,1,8,128]{3,0,2,1:T(8,128)S(1)}, f32[32,1,8,128]{3,0,2,1:T(8,128)S(1)}, u32[]{:S(2)}, u32[]{:S(2)}) collective-permute-start(f32[32,1,8,128]{3,0,2,1:T(8,128)S(1)} %broadcast.66), channel_id=1, source_target_pairs={{8,0},{16,8},{24,16},{9,1},{17,9},{25,17},{10,2},{18,10},{26,18},{... | collective-permute-start | bytes 393224 | tf_op jit(solution)/shard_map/ppermute | solution.py:43
  8.5 43.7 %collective-permute-start.1 = (f32[32,1,8,128]{3,0,2,1:T(8,128)S(1)}, f32[32,1,8,128]{3,0,2,1:T(8,128)S(1)}, u32[]{:S(2)}, u32[]{:S(2)}) collective-permute-start(f32[32,1,8,128]{3,0,2,1:T(8,128)S(1)} %broadcast.66), channel_id=1, source_target_pairs={{0,8},{8,16},{16,24},{1,9},{9,17},{17,25},{2,10},{10,18},{18,26},{... | collective-permute-start | bytes 393224 | tf_op jit(solution)/shard_map/ppermute | solution.py:42
  63.3 24.1 %collective-permute-start.4 = (f32[32,10,10,1]{0,2,3,1:T(8,128)S(1)}, f32[32,10,10,1]{0,2,3,1:T(8,128)S(1)}, u32[]{:S(2)}, u32[]{:S(2)}) collective-permute-start(f32[32,10,10,1]{0,2,3,1:T(8,128)S(1)} %copy.75), channel_id=1, source_target_pairs={{1,0},{2,1},{3,2},{5,4},{6,5},{7,6},{9,8},{10,9},{11,10},{13,12},{... | collective-permute-start | bytes 38408 | tf_op jit(solution)/shard_map/ppermute | solution.py:43
  67.1 22.3 %collective-permute-start.5 = (f32[32,10,10,1]{0,2,3,1:T(8,128)S(1)}, f32[32,10,10,1]{0,2,3,1:T(8,128)S(1)}, u32[]{:S(2)}, u32[]{:S(2)}) collective-permute-start(f32[32,10,10,1]{0,2,3,1:T(8,128)S(1)} %copy.77), channel_id=1, source_target_pairs={{0,1},{1,2},{2,3},{4,5},{5,6},{6,7},{8,9},{9,10},{10,11},{12,13},{... | collective-permute-start | bytes 38408 | tf_op jit(solution)/shard_map/ppermute | solution.py:42
  94.1 7.8 %collective-permute-start.6 = (f32[32,1,8,128]{3,0,2,1:T(8,128)S(1)}, f32[32,1,8,128]{3,0,2,1:T(8,128)S(1)}, u32[]{:S(2)}, u32[]{:S(2)}) collective-permute-start(f32[32,1,8,128]{3,0,2,1:T(8,128)S(1)} %get-tuple-element.51), channel_id=1, source_target_pairs={{8,0},{16,8},{24,16},{9,1},{17,9},{25,17},{10,2},{18,10},{26,18},{... | collective-permute-start | bytes 393224 | tf_op jit(solution)/shard_map/ppermute | solution.py:43
  95.4 7.7 %collective-permute-start.7 = (f32[32,1,8,128]{3,0,2,1:T(8,128)S(1)}, f32[32,1,8,128]{3,0,2,1:T(8,128)S(1)}, u32[]{:S(2)}, u32[]{:S(2)}) collective-permute-start(f32[32,1,8,128]{3,0,2,1:T(8,128)S(1)} %get-tuple-element.50), channel_id=1, source_target_pairs={{0,8},{8,16},{16,24},{1,9},{9,17},{17,25},{2,10},{10,18},{18,26},{... | collective-permute-start | bytes 393224 | tf_op jit(solution)/shard_map/ppermute | solution.py:42
  113.3 8.3 %collective-permute-start.10 = (f32[32,10,10,1]{0,2,3,1:T(8,128)S(1)}, f32[32,10,10,1]{0,2,3,1:T(8,128)S(1)}, u32[]{:S(2)}, u32[]{:S(2)}) collective-permute-start(f32[32,10,10,1]{0,2,3,1:T(8,128)S(1)} %copy.80), channel_id=1, source_target_pairs={{1,0},{2,1},{3,2},{5,4},{6,5},{7,6},{9,8},{10,9},{11,10},{13,12},{... | collective-permute-start | bytes 38408 | tf_op jit(solution)/shard_map/ppermute | solution.py:43
  128.4 7.9 %collective-permute-start.12 = (f32[32,1,8,128]{3,0,2,1:T(8,128)S(1)}, f32[32,1,8,128]{3,0,2,1:T(8,128)S(1)}, u32[]{:S(2)}, u32[]{:S(2)}) collective-permute-start(f32[32,1,8,128]{3,0,2,1:T(8,128)S(1)} %get-tuple-element.49), channel_id=1, source_target_pairs={{8,0},{16,8},{24,16},{9,1},{17,9},{25,17},{10,2},{18,10},{26,18},{... | collective-permute-start | bytes 393224 | tf_op jit(solution)/shard_map/ppermute | solution.py:43
  129.7 7.8 %collective-permute-start.13 = (f32[32,1,8,128]{3,0,2,1:T(8,128)S(1)}, f32[32,1,8,128]{3,0,2,1:T(8,128)S(1)}, u32[]{:S(2)}, u32[]{:S(2)}) collective-permute-start(f32[32,1,8,128]{3,0,2,1:T(8,128)S(1)} %get-tuple-element.48), channel_id=1, source_target_pairs={{0,8},{8,16},{16,24},{1,9},{9,17},{17,25},{2,10},{10,18},{18,26},{... | collective-permute-start | bytes 393224 | tf_op jit(solution)/shard_map/ppermute | solution.py:42
  148.4 7.3 %collective-permute-start.16 = (f32[32,10,10,1]{0,2,3,1:T(8,128)S(1)}, f32[32,10,10,1]{0,2,3,1:T(8,128)S(1)}, u32[]{:S(2)}, u32[]{:S(2)}) collective-permute-start(f32[32,10,10,1]{0,2,3,1:T(8,128)S(1)} %copy.85), channel_id=1, source_target_pairs={{1,0},{2,1},{3,2},{5,4},{6,5},{7,6},{9,8},{10,9},{11,10},{13,12},{... | collective-permute-start | bytes 38408 | tf_op jit(solution)/shard_map/ppermute | solution.py:43
  150.7 7.2 %collective-permute-start.17 = (f32[32,10,10,1]{0,2,3,1:T(8,128)S(1)}, f32[32,10,10,1]{0,2,3,1:T(8,128)S(1)}, u32[]{:S(2)}, u32[]{:S(2)}) collective-permute-start(f32[32,10,10,1]{0,2,3,1:T(8,128)S(1)} %copy.87), channel_id=1, source_target_pairs={{0,1},{1,2},{2,3},{4,5},{5,6},{6,7},{8,9},{9,10},{10,11},{12,13},{... | collective-permute-start | bytes 38408 | tf_op jit(solution)/shard_map/ppermute | solution.py:42
  162.8 8.7 %collective-permute-start.18 = (f32[32,1,8,128]{3,0,2,1:T(8,128)S(1)}, f32[32,1,8,128]{3,0,2,1:T(8,128)S(1)}, u32[]{:S(2)}, u32[]{:S(2)}) collective-permute-start(f32[32,1,8,128]{3,0,2,1:T(8,128)S(1)} %get-tuple-element.47), channel_id=1, source_target_pairs={{8,0},{16,8},{24,16},{9,1},{17,9},{25,17},{10,2},{18,10},{26,18},{... | collective-permute-start | bytes 393224 | tf_op jit(solution)/shard_map/ppermute | solution.py:43
  164.1 8.5 %collective-permute-start.19 = (f32[32,1,8,128]{3,0,2,1:T(8,128)S(1)}, f32[32,1,8,128]{3,0,2,1:T(8,128)S(1)}, u32[]{:S(2)}, u32[]{:S(2)}) collective-permute-start(f32[32,1,8,128]{3,0,2,1:T(8,128)S(1)} %get-tuple-element.46), channel_id=1, source_target_pairs={{0,8},{8,16},{16,24},{1,9},{9,17},{17,25},{2,10},{10,18},{18,26},{... | collective-permute-start | bytes 393224 | tf_op jit(solution)/shard_map/ppermute | solution.py:42
  183.3 8.6 %collective-permute-start.22 = (f32[32,10,10,1]{0,2,3,1:T(8,128)S(1)}, f32[32,10,10,1]{0,2,3,1:T(8,128)S(1)}, u32[]{:S(2)}, u32[]{:S(2)}) collective-permute-start(f32[32,10,10,1]{0,2,3,1:T(8,128)S(1)} %copy.90), channel_id=1, source_target_pairs={{1,0},{2,1},{3,2},{5,4},{6,5},{7,6},{9,8},{10,9},{11,10},{13,12},{... | collective-permute-start | bytes 38408 | tf_op jit(solution)/shard_map/ppermute | solution.py:43
  238.3 72.8 %all-gather.2.cloned.1.call-start = ((), (), s32[]{:S(2)}) async-start(), calls=%async_computation.3 | async-start | bytes 1310720 | tf_op jit(solution)/shard_map/all_gather | solution.py:122
  278.4 259.3 %reduce-scatter.5.cloned.1.call-start = ((), (), s32[]{:S(2)}) async-start(), calls=%async_computation.4 | async-start | bytes 2621440 | tf_op jit(solution)/shard_map/reduce_scatter | solution.py:118
  297.1 7.3 %collective-permute-start.29 = (f32[32,10,10,1]{0,2,3,1:T(8,128)S(1)}, f32[32,10,10,1]{0,2,3,1:T(8,128)S(1)}, u32[]{:S(2)}, u32[]{:S(2)}) collective-permute-start(f32[32,10,10,1]{0,2,3,1:T(8,128)S(1)} %copy.100), channel_id=1, source_target_pairs={{0,1},{1,2},{2,3},{4,5},{5,6},{6,7},{8,9},{9,10},{10,11},{12,13},{... | collective-permute-start | bytes 38408 | tf_op jit(solution)/shard_map/ppermute | solution.py:42
  353.7 9.2 %collective-permute-start.30 = (f32[32,1,8,128]{3,0,2,1:T(8,128)S(1)}, f32[32,1,8,128]{3,0,2,1:T(8,128)S(1)}, u32[]{:S(2)}, u32[]{:S(2)}) collective-permute-start(f32[32,1,8,128]{3,0,2,1:T(8,128)S(1)} %get-tuple-element.43), channel_id=1, source_target_pairs={{8,0},{16,8},{24,16},{9,1},{17,9},{25,17},{10,2},{18,10},{26,18},{... | collective-permute-start | bytes 393224 | tf_op jit(solution)/shard_map/ppermute | solution.py:43
  355.0 9.1 %collective-permute-start.31 = (f32[32,1,8,128]{3,0,2,1:T(8,128)S(1)}, f32[32,1,8,128]{3,0,2,1:T(8,128)S(1)}, u32[]{:S(2)}, u32[]{:S(2)}) collective-permute-start(f32[32,1,8,128]{3,0,2,1:T(8,128)S(1)} %get-tuple-element.42), channel_id=1, source_target_pairs={{0,8},{8,16},{16,24},{1,9},{9,17},{17,25},{2,10},{10,18},{18,26},{... | collective-permute-start | bytes 393224 | tf_op jit(solution)/shard_map/ppermute | solution.py:42
  374.4 8.3 %collective-permute-start.34 = (f32[32,10,10,1]{0,2,3,1:T(8,128)S(1)}, f32[32,10,10,1]{0,2,3,1:T(8,128)S(1)}, u32[]{:S(2)}, u32[]{:S(2)}) collective-permute-start(f32[32,10,10,1]{0,2,3,1:T(8,128)S(1)} %copy.103), channel_id=1, source_target_pairs={{1,0},{2,1},{3,2},{5,4},{6,5},{7,6},{9,8},{10,9},{11,10},{13,12},{... | collective-permute-start | bytes 38408 | tf_op jit(solution)/shard_map/ppermute | solution.py:43
  389.5 8.6 %collective-permute-start.36 = (f32[32,1,8,128]{3,0,2,1:T(8,128)S(1)}, f32[32,1,8,128]{3,0,2,1:T(8,128)S(1)}, u32[]{:S(2)}, u32[]{:S(2)}) collective-permute-start(f32[32,1,8,128]{3,0,2,1:T(8,128)S(1)} %get-tuple-element.41), channel_id=1, source_target_pairs={{8,0},{16,8},{24,16},{9,1},{17,9},{25,17},{10,2},{18,10},{26,18},{... | collective-permute-start | bytes 393224 | tf_op jit(solution)/shard_map/ppermute | solution.py:43
  390.8 8.4 %collective-permute-start.37 = (f32[32,1,8,128]{3,0,2,1:T(8,128)S(1)}, f32[32,1,8,128]{3,0,2,1:T(8,128)S(1)}, u32[]{:S(2)}, u32[]{:S(2)}) collective-permute-start(f32[32,1,8,128]{3,0,2,1:T(8,128)S(1)} %get-tuple-element.40), channel_id=1, source_target_pairs={{0,8},{8,16},{16,24},{1,9},{9,17},{17,25},{2,10},{10,18},{18,26},{... | collective-permute-start | bytes 393224 | tf_op jit(solution)/shard_map/ppermute | solution.py:42
  410.1 7.4 %collective-permute-start.40 = (f32[32,10,10,1]{0,2,3,1:T(8,128)S(1)}, f32[32,10,10,1]{0,2,3,1:T(8,128)S(1)}, u32[]{:S(2)}, u32[]{:S(2)}) collective-permute-start(f32[32,10,10,1]{0,2,3,1:T(8,128)S(1)} %copy.108), channel_id=1, source_target_pairs={{1,0},{2,1},{3,2},{5,4},{6,5},{7,6},{9,8},{10,9},{11,10},{13,12},{... | collective-permute-start | bytes 38408 | tf_op jit(solution)/shard_map/ppermute | solution.py:43
  412.4 7.3 %collective-permute-start.41 = (f32[32,10,10,1]{0,2,3,1:T(8,128)S(1)}, f32[32,10,10,1]{0,2,3,1:T(8,128)S(1)}, u32[]{:S(2)}, u32[]{:S(2)}) collective-permute-start(f32[32,10,10,1]{0,2,3,1:T(8,128)S(1)} %copy.110), channel_id=1, source_target_pairs={{0,1},{1,2},{2,3},{4,5},{5,6},{6,7},{8,9},{9,10},{10,11},{12,13},{... | collective-permute-start | bytes 38408 | tf_op jit(solution)/shard_map/ppermute | solution.py:42
  424.5 8.7 %collective-permute-start.42 = (f32[32,1,8,128]{3,0,2,1:T(8,128)S(1)}, f32[32,1,8,128]{3,0,2,1:T(8,128)S(1)}, u32[]{:S(2)}, u32[]{:S(2)}) collective-permute-start(f32[32,1,8,128]{3,0,2,1:T(8,128)S(1)} %get-tuple-element.39), channel_id=1, source_target_pairs={{8,0},{16,8},{24,16},{9,1},{17,9},{25,17},{10,2},{18,10},{26,18},{... | collective-permute-start | bytes 393224 | tf_op jit(solution)/shard_map/ppermute | solution.py:43
  425.8 8.5 %collective-permute-start.43 = (f32[32,1,8,128]{3,0,2,1:T(8,128)S(1)}, f32[32,1,8,128]{3,0,2,1:T(8,128)S(1)}, u32[]{:S(2)}, u32[]{:S(2)}) collective-permute-start(f32[32,1,8,128]{3,0,2,1:T(8,128)S(1)} %get-tuple-element.38), channel_id=1, source_target_pairs={{0,8},{8,16},{16,24},{1,9},{9,17},{17,25},{2,10},{10,18},{18,26},{... | collective-permute-start | bytes 393224 | tf_op jit(solution)/shard_map/ppermute | solution.py:42
  444.6 8.6 %collective-permute-start.46 = (f32[32,10,10,1]{0,2,3,1:T(8,128)S(1)}, f32[32,10,10,1]{0,2,3,1:T(8,128)S(1)}, u32[]{:S(2)}, u32[]{:S(2)}) collective-permute-start(f32[32,10,10,1]{0,2,3,1:T(8,128)S(1)} %copy.113), channel_id=1, source_target_pairs={{1,0},{2,1},{3,2},{5,4},{6,5},{7,6},{9,8},{10,9},{11,10},{13,12},{... | collective-permute-start | bytes 38408 | tf_op jit(solution)/shard_map/ppermute | solution.py:43
  448.3 7.1 %collective-permute-start.47 = (f32[32,10,10,1]{0,2,3,1:T(8,128)S(1)}, f32[32,10,10,1]{0,2,3,1:T(8,128)S(1)}, u32[]{:S(2)}, u32[]{:S(2)}) collective-permute-start(f32[32,10,10,1]{0,2,3,1:T(8,128)S(1)} %copy.115), channel_id=1, source_target_pairs={{0,1},{1,2},{2,3},{4,5},{5,6},{6,7},{8,9},{9,10},{10,11},{12,13},{... | collective-permute-start | bytes 38408 | tf_op jit(solution)/shard_map/ppermute | solution.py:42
  538.9 14.5 %collective-permute-start.48 = (f32[32,4096]{1,0:T(8,128)S(1)}, f32[32,4096]{1,0:T(8,128)S(1)}, u32[]{:S(2)}, u32[]{:S(2)}) collective-permute-start(f32[32,4096]{1,0:T(8,128)S(1)} %multiply_add_fusion), channel_id=1, source_target_pairs={{0,8},{8,16},{16,24},{24,0},{1,9},{9,17},{17,25},{25,1},{2,10},{10... | collective-permute-start | bytes 1572872 | tf_op jit(solution)/shard_map/ppermute | solution.py:25
  553.4 13.5 %collective-permute-start.49 = (f32[32,4096]{1,0:T(8,128)S(1)}, f32[32,4096]{1,0:T(8,128)S(1)}, u32[]{:S(2)}, u32[]{:S(2)}) collective-permute-start(f32[32,4096]{1,0:T(8,128)S(1)} %collective-permute-done.48), channel_id=1, source_target_pairs={{0,8},{8,16},{16,24},{24,0},{1,9},{9,17},{17,25},{25,1},{2,10},{10... | collective-permute-start | bytes 1572872 | tf_op jit(solution)/shard_map/ppermute | solution.py:25
  566.9 12.7 %collective-permute-start.50 = (f32[32,4096]{1,0:T(8,128)S(1)}, f32[32,4096]{1,0:T(8,128)S(1)}, u32[]{:S(2)}, u32[]{:S(2)}) collective-permute-start(f32[32,4096]{1,0:T(8,128)S(1)} %collective-permute-done.49), channel_id=1, source_target_pairs={{0,8},{8,16},{16,24},{24,0},{1,9},{9,17},{17,25},{25,1},{2,10},{10... | collective-permute-start | bytes 1572872 | tf_op jit(solution)/shard_map/ppermute | solution.py:25
  (47 other events, 249.7 us)
Sparse Core Ops, SparseCore 0:
  238.4 37.9 reduce-scatter.2
  278.8 26.9 all-gather.1
  499.7 37.9 reduce-scatter.4
